TPU v7x, 256 devices: a whole 4x4x8 slice. The times are simulated.
256 devices in a mesh: sx: 8 (over z_hi, x), sy: 4 (over z_lo), af: 8 (over y, core).
Axes of the slice: x: 4, y: 4, z: 8 (z_hi: 2, z_lo: 4; z = z_hi * 4 + z_lo), core: 2. Of those that a mesh axis runs over, the one named last changes fastest.
Arguments:
- volume: bfloat16 [8, 48, 48, 48, 128], P('af', 'sx', 'sy'), may hold values from -6 to 6
- kernel: bfloat16 [3, 3, 3, 128, 256], P(None, None, None, 'sx', ('sy', 'af')), may hold values from -0.109375 to 0.109375
- cotangent: bfloat16 [8, 256, 24, 576], P('sx', ('sy', 'af')), may hold values from -6 to 6
Outputs:
- features: bfloat16 [8, 256, 24, 576], P('sx', ('sy', 'af'))
- volume_grad: bfloat16 [8, 48, 48, 48, 128], P('af', 'sx', 'sy')
- kernel_grad: float32 [3, 3, 3, 128, 256], P(None, None, None, 'sx', ('sy', 'af'))
All inputs are finite; a program needn't handle non-finite values.
Results may differ from a plain program's by a relative error of at most 0.0025.
Values may be sent and summed in bfloat16 or wider, within the bound.
A program may use at most 64 MiB of HBM per device.

v0:
```python
import jax
import jax.numpy as jnp
from jax import lax
from jax.sharding import PartitionSpec as P


def from_behind(value, axis, steps):
    count = lax.axis_size(axis)
    leading, last = (max(0, -steps), min(count, count - steps))
    return lax.ppermute(value, axis, [(source, source + steps) for source in range(leading, last)])


def strided_patch(extended, tap_d, tap_h, tap_w, depth, height, width):
    return extended[
        :,
        tap_d : tap_d + 2 * depth : 2,
        tap_h : tap_h + 2 * height : 2,
        tap_w : tap_w + 2 * width : 2,
        :,
    ]


def parity_view(extended):
    samples, d_ext, h_ext, w_ext, channels = extended.shape
    pads = [(0, 0)] + [(0, n % 2) for n in (d_ext, h_ext, w_ext)] + [(0, 0)]
    even = jnp.pad(extended, pads)
    _, d2, h2, w2, _ = even.shape
    split = even.reshape(samples, d2 // 2, 2, h2 // 2, 2, w2 // 2, 2, channels)
    return split.transpose(2, 4, 6, 0, 1, 3, 5, 7)


def im2col(classes, depth, height, width):
    patches = []
    for tap_d in range(3):
        for tap_h in range(3):
            for tap_w in range(3):
                cls = classes[tap_d % 2, tap_h % 2, tap_w % 2]
                od, oh, ow = (tap_d // 2, tap_h // 2, tap_w // 2)
                patches.append(cls[:, od : od + depth, oh : oh + height, ow : ow + width, :])
    return jnp.concatenate(patches, axis=-1)


def weave(even_part, odd_part, axis):
    stacked = jnp.stack([even_part, odd_part], axis=axis + 1)
    shape = list(even_part.shape)
    shape[axis] = shape[axis] * 2
    return stacked.reshape(shape)


def spread_back(grad_space, kernel_full):
    samples, depth, height, width, filters = grad_space.shape
    channels = kernel_full.shape[3]
    grad_flat = grad_space.reshape(-1, filters)
    classes = {}
    for tap_d in range(3):
        for tap_h in range(3):
            for tap_w in range(3):
                term = lax.dot_general(
                    grad_flat,
                    kernel_full[tap_d, tap_h, tap_w],
                    (((1,), (1,)), ((), ())),
                    preferred_element_type=jnp.float32,
                )
                term = term.reshape(samples, depth, height, width, channels)
                pads = [(0, 0)]
                for tap in (tap_d, tap_h, tap_w):
                    pads.append((1, 0) if tap == 2 else (0, 1))
                pads.append((0, 0))
                term = jnp.pad(term, pads)
                key_name = (tap_d % 2, tap_h % 2, tap_w % 2)
                classes[key_name] = classes[key_name] + term if key_name in classes else term
    planes = []
    for parity_d in range(2):
        rows_h = []
        for parity_h in range(2):
            rows_h.append(weave(classes[parity_d, parity_h, 0], classes[parity_d, parity_h, 1], 3))
        planes.append(weave(rows_h[0], rows_h[1], 2))
    whole = weave(planes[0], planes[1], 1)
    return whole[:, : 2 * depth + 1, : 2 * height + 1, : 2 * width + 1, :]


def on_device(volume, kernel, cotangent):
    samples = volume.shape[0]
    depth = volume.shape[1] // 2
    height = volume.shape[2] // 2
    width = volume.shape[3] // 2
    n_sy = lax.axis_size("sy")
    n_af = lax.axis_size("af")
    kernel_part = lax.all_gather(kernel, ("sy", "af"), axis=4, tiled=True)
    kernel_full = lax.all_gather(kernel_part, "sx", axis=3, tiled=True)
    filters = kernel_full.shape[4]
    per_dev = filters // (n_sy * n_af)
    below = from_behind(volume[:, -1:], "sx", 1)
    extended = jnp.concatenate([below, volume], axis=1)
    beside = from_behind(extended[:, :, -1:], "sy", 1)
    extended = jnp.concatenate([beside, extended], axis=2)
    extended = jnp.pad(extended, ((0, 0), (0, 0), (0, 0), (1, 0), (0, 0)))
    rows = samples * depth * height * width
    classes = parity_view(extended)
    cols = im2col(classes, depth, height, width).reshape(rows, -1)
    kernel_mat = kernel_full.reshape(-1, filters)
    total = jnp.dot(cols, kernel_mat, preferred_element_type=jnp.float32)
    conv_space = total.astype(jnp.bfloat16).reshape(
        samples, depth, height, width, n_sy, n_af, per_dev
    )
    by_sample = lax.all_to_all(conv_space, "af", split_axis=5, concat_axis=0, tiled=True)
    gathered = lax.all_to_all(
        lax.all_to_all(by_sample, "sx", split_axis=0, concat_axis=1, tiled=True),
        "sy",
        split_axis=4,
        concat_axis=2,
        tiled=True,
    )
    own_samples = gathered.shape[0]
    edge_d = gathered.shape[1]
    edge_h = gathered.shape[2]
    features = (
        gathered.reshape(own_samples, edge_d, edge_h, width, per_dev)
        .transpose(0, 4, 1, 2, 3)
        .reshape(own_samples, per_dev, edge_d, edge_h * width)
    )
    grad_after = (
        cotangent.reshape(own_samples, per_dev, edge_d, edge_h, width)
        .transpose(0, 2, 3, 4, 1)
        .reshape(own_samples, edge_d, edge_h, width, 1, 1, per_dev)
    )
    grad_region = lax.all_to_all(
        lax.all_to_all(grad_after, "sx", split_axis=1, concat_axis=0, tiled=True),
        "sy",
        split_axis=2,
        concat_axis=4,
        tiled=True,
    )
    grad_back = lax.all_to_all(grad_region, "af", split_axis=0, concat_axis=5, tiled=True)
    grad_space = grad_back.reshape(samples, depth, height, width, filters)
    grad_flat = grad_space.reshape(rows, filters)
    kernel_terms = lax.dot_general(
        cols, grad_flat, (((0,), (0,)), ((), ())), preferred_element_type=jnp.float32
    )
    n_sx = lax.axis_size("sx")
    channels = kernel_full.shape[3]
    taps = kernel_terms.reshape(27, channels, n_sy * n_af, per_dev).transpose(2, 0, 1, 3)
    by_filter = lax.all_to_all(taps, ("sy", "af"), 0, 0, tiled=True).sum(axis=0)
    own_ch = channels // n_sx
    by_filter = by_filter.reshape(27, n_sx, own_ch, per_dev).transpose(1, 0, 2, 3)
    kernel_grad = lax.all_to_all(by_filter, "sx", 0, 0, tiled=True).sum(axis=0)
    kernel_grad = kernel_grad.reshape(3, 3, 3, own_ch, per_dev)
    partial_grad = spread_back(grad_space, kernel_full)
    from_above = from_behind(partial_grad[:, 0:1], "sx", -1)
    own_depth = partial_grad[:, 1:]
    own_depth = jnp.concatenate([own_depth[:, :-1], own_depth[:, -1:] + from_above], axis=1)
    from_right = from_behind(own_depth[:, :, 0:1].astype(jnp.bfloat16), "sy", -1).astype(
        jnp.float32
    )
    own_height = own_depth[:, :, 1:]
    own_height = jnp.concatenate(
        [own_height[:, :, :-1], own_height[:, :, -1:] + from_right], axis=2
    )
    volume_grad = own_height[:, :, :, 1:]
    return (features, volume_grad.astype(jnp.bfloat16), kernel_grad)


def solution(mesh):
    return jax.shard_map(
        on_device,
        mesh=mesh,
        in_specs=(
            P("af", "sx", "sy", None, None),
            P(None, None, None, "sx", ("sy", "af")),
            P("sx", ("sy", "af"), None, None),
        ),
        out_specs=(
            P("sx", ("sy", "af"), None, None),
            P("af", "sx", "sy", None, None),
            P(None, None, None, "sx", ("sy", "af")),
        ),
        check_vma=False,
    )
```

profile of v0, /device:TPU:96, one launch (start us, length us, event | category | flops | bytes accessed | tf_op | source)
XLA Modules:
  0.0 357.8 jit_solution(4887128388619679048)
XLA Ops:
  9.3 3.4 collective-permute-start
  12.8 6.2 %collective-permute-done = bf16[1,1,12,48,128]{4,1,3,2,0:T(2,128)(2,1)S(1)} collective-permute-done((bf16[1,1,12,48,128]{4,1,3,2,0:T(2,128)(2,1)S(1)}, bf16[1,1,12,48,128]{4,1,3,2,0:T(2,128)(2,1)S(1)}, u32[]{:S(2)}, u32[]{:S(2)}) %collective-permute-start) | collective-permute-done | bytes 147488 | tf_op jit(solution)/shard_map/ppermute | solution.py:10
  21.0 40.2 %all_gather.6 = bf16[3,3,3,16,256]{3,4,2,1,0:T(8,128)(2,1)S(1)} all-gather(bf16[3,3,3,16,8]{3,4,2,1,0:T(8,128)(2,1)S(1)} %copy-done.8), channel_id=1, replica_groups=mesh['sx'=8,'sy'=4,'af'=8] {'sy','af'}, dimensions={4}, use_global_device_ids=true | all-gather | bytes 228096 | tf_op jit(solution)/shard_map/all_gather | solution.py:89
  67.7 18.5 %all-to-all-start.3 = ((bf16[8,2,6912]{2,1,0:T(2,128)(2,1)}), bf16[8,2,6912]{2,1,0:T(2,128)(2,1)S(1)}, u32[]{:S(2)}, u32[]{:S(2)}) async-start(bf16[8,2,6912]{2,1,0:T(2,128)(2,1)} %reshape.261), calls=%async_computation.3 | async-start | bytes 442368 | tf_op jit(solution)/shard_map/all_to_all | solution.py:128
  112.7 12.0 %all-to-all-start.4 = ((bf16[4,2,13824]{2,1,0:T(2,128)(2,1)}), bf16[4,2,13824]{2,1,0:T(2,128)(2,1)S(1)}, u32[]{:S(2)}, u32[]{:S(2)}) async-start(bf16[4,2,13824]{2,1,0:T(2,128)(2,1)} %reshape.263), calls=%async_computation.4 | async-start | bytes 442368 | tf_op jit(solution)/shard_map/all_to_all | solution.py:127
  126.2 10.7 %all-to-all-done.4 = bf16[4,2,13824]{2,1,0:T(2,128)(2,1)S(1)} async-done(((bf16[4,2,13824]{2,1,0:T(2,128)(2,1)}), bf16[4,2,13824]{2,1,0:T(2,128)(2,1)S(1)}, u32[]{:S(2)}, u32[]{:S(2)}) %all-to-all-start.4) | async-done | bytes 221216 | tf_op jit(solution)/shard_map/all_to_all | solution.py:127
  141.2 8.3 %all-to-all-start.5 = ((bf16[8,2,6912]{2,1,0:T(2,128)(2,1)}), bf16[8,2,6912]{2,1,0:T(2,128)(2,1)}, u32[]{:S(2)}, u32[]{:S(2)}) async-start(bf16[8,2,6912]{2,1,0:T(2,128)(2,1)} %reshape.265), calls=%async_computation.5 | async-start | bytes 442368 | tf_op jit(solution)/shard_map/all_to_all | solution.py:134
  150.2 4.0 %copy.581 = bf16[1,3,6,24,3456]{4,3,2,1,0:T(8,128)(2,1)} copy(bf16[1,3,6,24,3456]{4,1,3,2,0:T(4,128)(2,1)} %slice_dynamic-update-slice_fusion) | data formatting | bytes 5971968 | tf_op jit(solution)/shard_map/concatenate | solution.py:40
  154.2 4.3 %dot_general.205 = bf16[27,128,432]{1,0,2:T(8,128)(2,1)S(1)} reshape(bf16[3456,432]{0,1:T(8,128)(2,1)} %bitcast.438) | data formatting | bytes 5971968 | tf_op jit(solution)/shard_map/dot_general | solution.py:137
  158.5 3.6 %reshape.266 = bf16[8,1,3,4,6,8,24]{6,5,4,3,2,1,0:T(8,128)(2,1)} reshape(bf16[8,2,6912]{2,1,0:T(2,128)(2,1)} %all-to-all-done.5) | data formatting | bytes 442368
  162.2 4.0 %convolution_convert_fusion = bf16[432,256]{1,0:T(8,128)(2,1)} fusion(bf16[432,3456]{1,0:T(8,128)(2,1)} %bitcast.439, bf16[3456,256]{1,0:T(8,128)(2,1)} %bitcast.458), kind=kOutput, calls=%fused_computation.16 | convolution fusion | flops 764522496 | bytes 4976640 | tf_op jit(solution)/shard_map/dot_general | solution.py:102
  173.5 3.5 reshape.255
  177.0 4.8 %all-to-all-start = ((bf16[8,2,6912]{2,1,0:T(2,128)(2,1)}), bf16[8,2,6912]{2,1,0:T(2,128)(2,1)}, u32[]{:S(2)}, u32[]{:S(2)}) async-start(bf16[8,2,6912]{2,1,0:T(2,128)(2,1)} %reshape.255), calls=%async_computation | async-start | bytes 442368 | tf_op jit(solution)/shard_map/all_to_all | solution.py:106
  189.0 3.6 %reshape.256 = bf16[8,1,3,6,4,8,24]{6,5,4,3,2,1,0:T(8,128)(2,1)} reshape(bf16[8,2,6912]{2,1,0:T(2,128)(2,1)} %all-to-all-done) | data formatting | bytes 442368
  195.2 3.5 reshape.257
  198.7 9.4 %all-to-all-start.1 = ((bf16[8,2,6912]{2,1,0:T(2,128)(2,1)}), bf16[8,2,6912]{2,1,0:T(2,128)(2,1)}, u32[]{:S(2)}, u32[]{:S(2)}) async-start(bf16[8,2,6912]{2,1,0:T(2,128)(2,1)} %reshape.257), calls=%async_computation.1 | async-start | bytes 442368 | tf_op jit(solution)/shard_map/all_to_all | solution.py:108
  210.4 3.9 %copy.631 = f32[32,27,128,8]{2,3,1,0:T(8,128)} copy(f32[32,27,128,8]{2,0,3,1:T(8,128)S(1)} %fusion.6) | data formatting | bytes 7077888 | tf_op jit(solution)/shard_map/transpose | solution.py:142
  214.2 4.9 %all-to-all-done.1 = bf16[8,2,6912]{2,1,0:T(2,128)(2,1)} async-done(((bf16[8,2,6912]{2,1,0:T(2,128)(2,1)}), bf16[8,2,6912]{2,1,0:T(2,128)(2,1)}, u32[]{:S(2)}, u32[]{:S(2)}) %all-to-all-start.1) | async-done | bytes 221216 | tf_op jit(solution)/shard_map/all_to_all | solution.py:108
  219.1 8.7 %all-to-all-start.6 = ((f32[32,27,128,8]{2,3,1,0:T(8,128)}), f32[32,27,128,8]{2,3,1,0:T(8,128)}, u32[]{:S(2)}, u32[]{:S(2)}) async-start(f32[32,27,128,8]{2,3,1,0:T(8,128)} %copy.631), calls=%async_computation.6 | async-start | bytes 7077888 | tf_op jit(solution)/shard_map/all_to_all | solution.py:143
  249.8 3.6 %reshape.258 = bf16[8,3,6,4,1,8,24]{6,5,4,3,2,1,0:T(8,128)(2,1)} reshape(bf16[8,2,6912]{2,1,0:T(2,128)(2,1)} %all-to-all-done.1) | data formatting | bytes 442368
  256.0 3.5 reshape.259
  259.5 53.2 %all-to-all-done.6 = f32[32,27,128,8]{2,3,1,0:T(8,128)} async-done(((f32[32,27,128,8]{2,3,1,0:T(8,128)}), f32[32,27,128,8]{2,3,1,0:T(8,128)}, u32[]{:S(2)}, u32[]{:S(2)}) %all-to-all-start.6) | async-done | bytes 3538976 | tf_op jit(solution)/shard_map/all_to_all | solution.py:143
  312.7 5.9 %all-to-all-start.2 = ((bf16[4,2,13824]{2,1,0:T(2,128)(2,1)}), bf16[4,2,13824]{2,1,0:T(2,128)(2,1)}, u32[]{:S(2)}, u32[]{:S(2)}) async-start(bf16[4,2,13824]{2,1,0:T(2,128)(2,1)} %reshape.259), calls=%async_computation.2 | async-start | bytes 442368 | tf_op jit(solution)/shard_map/all_to_all | solution.py:107
  334.1 3.6 %all-to-all-start.7 = ((f32[8,1,3456]{2,1,0:T(1,128)}), f32[8,1,3456]{2,1,0:T(1,128)S(1)}, u32[]{:S(2)}, u32[]{:S(2)}) async-start(f32[8,1,3456]{2,1,0:T(1,128)} %reshape.267), calls=%async_computation.7 | async-start | bytes 221184 | tf_op jit(solution)/shard_map/all_to_all | solution.py:146
  (156 shorter events, 115.6 us)
Async XLA Ops:
  7.2 13.9 %copy-start.8 = (bf16[3,3,3,16,8]{3,4,2,1,0:T(8,128)(2,1)S(1)}, bf16[3,3,3,16,8]{3,4,2,1,0:T(8,128)(2,1)}, u32[]{:S(2)}) copy-start(bf16[3,3,3,16,8]{3,4,2,1,0:T(8,128)(2,1)} %param.4) | copy-start | bytes 20740
  7.2 155.0 %all-gather.2.cloned.1.call-start = ((), (), s32[]{:S(2)}) async-start(), calls=%async_computation.8 | async-start | bytes 1990656 | tf_op jit(solution)/shard_map/all_gather | solution.py:90
  9.3 9.7 %collective-permute-start = (bf16[1,1,12,48,128]{4,1,3,2,0:T(2,128)(2,1)S(1)}, bf16[1,1,12,48,128]{4,1,3,2,0:T(2,128)(2,1)S(1)}, u32[]{:S(2)}, u32[]{:S(2)}) collective-permute-start(bf16[1,1,12,48,128]{4,1,3,2,0:T(2,128)(2,1)S(1)} %slice.315), channel_id=1, source_target_pairs={{0,32},{32,64},{64,96},{96,128},{128,160},{160,192},{192,224},{1,3... | collective-permute-start | bytes 442376 | tf_op jit(solution)/shard_map/ppermute | solution.py:10
  19.0 0.7 copy-start.6
  19.7 66.5 %collective-permute-start.1 = (bf16[1,7,1,48,128]{4,1,3,2,0:T(8,128)(2,1)}, bf16[1,7,1,48,128]{4,1,3,2,0:T(8,128)(2,1)}, u32[]{:S(2)}, u32[]{:S(2)}) collective-permute-start(bf16[1,7,1,48,128]{4,1,3,2,0:T(8,128)(2,1)} %pad_maximum_fusion.9), channel_id=1, source_target_pairs={{0,8},{8,16},{16,24},{1,9},{9,17},{17,25},{2,10},{10,18},{18,26},{... | collective-permute-start | bytes 258056 | tf_op jit(solution)/shard_map/ppermute | solution.py:10
  65.5 20.7 %copy-start.7 = (bf16[1,1,12,48,128]{4,1,3,2,0:T(2,128)(2,1)S(1)}, bf16[1,1,12,48,128]{4,1,3,2,0:T(2,128)(2,1)}, u32[]{:S(2)}) copy-start(bf16[1,1,12,48,128]{4,1,3,2,0:T(2,128)(2,1)} %copy-done.6) | copy-start | bytes 442372
  67.7 40.8 %all-to-all-start.3 = ((bf16[8,2,6912]{2,1,0:T(2,128)(2,1)}), bf16[8,2,6912]{2,1,0:T(2,128)(2,1)S(1)}, u32[]{:S(2)}, u32[]{:S(2)}) async-start(bf16[8,2,6912]{2,1,0:T(2,128)(2,1)} %reshape.261), calls=%async_computation.3 | async-start | bytes 442368 | tf_op jit(solution)/shard_map/all_to_all | solution.py:128
  112.7 24.2 %all-to-all-start.4 = ((bf16[4,2,13824]{2,1,0:T(2,128)(2,1)}), bf16[4,2,13824]{2,1,0:T(2,128)(2,1)S(1)}, u32[]{:S(2)}, u32[]{:S(2)}) async-start(bf16[4,2,13824]{2,1,0:T(2,128)(2,1)} %reshape.263), calls=%async_computation.4 | async-start | bytes 442368 | tf_op jit(solution)/shard_map/all_to_all | solution.py:127
  141.2 17.4 %all-to-all-start.5 = ((bf16[8,2,6912]{2,1,0:T(2,128)(2,1)}), bf16[8,2,6912]{2,1,0:T(2,128)(2,1)}, u32[]{:S(2)}, u32[]{:S(2)}) async-start(bf16[8,2,6912]{2,1,0:T(2,128)(2,1)} %reshape.265), calls=%async_computation.5 | async-start | bytes 442368 | tf_op jit(solution)/shard_map/all_to_all | solution.py:134
  177.0 12.0 %all-to-all-start = ((bf16[8,2,6912]{2,1,0:T(2,128)(2,1)}), bf16[8,2,6912]{2,1,0:T(2,128)(2,1)}, u32[]{:S(2)}, u32[]{:S(2)}) async-start(bf16[8,2,6912]{2,1,0:T(2,128)(2,1)} %reshape.255), calls=%async_computation | async-start | bytes 442368 | tf_op jit(solution)/shard_map/all_to_all | solution.py:106
  183.2 1.0 copy-start.1
  198.7 20.4 %all-to-all-start.1 = ((bf16[8,2,6912]{2,1,0:T(2,128)(2,1)}), bf16[8,2,6912]{2,1,0:T(2,128)(2,1)}, u32[]{:S(2)}, u32[]{:S(2)}) async-start(bf16[8,2,6912]{2,1,0:T(2,128)(2,1)} %reshape.257), calls=%async_computation.1 | async-start | bytes 442368 | tf_op jit(solution)/shard_map/all_to_all | solution.py:108
  214.2 13.6 %copy-start.2 = (bf16[1,3,6,24,4,8,1,8]{3,7,2,4,1,5,6,0:T(8,128)(2,1)S(1)}, bf16[1,3,6,24,4,8,1,8]{3,7,2,4,1,5,6,0:T(8,128)(2,1)}, u32[]{:S(2)}) copy-start(bf16[1,3,6,24,4,8,1,8]{3,7,2,4,1,5,6,0:T(8,128)(2,1)} %copy-done.1) | copy-start | bytes 663556
  219.1 93.5 %all-to-all-start.6 = ((f32[32,27,128,8]{2,3,1,0:T(8,128)}), f32[32,27,128,8]{2,3,1,0:T(8,128)}, u32[]{:S(2)}, u32[]{:S(2)}) async-start(f32[32,27,128,8]{2,3,1,0:T(8,128)} %copy.631), calls=%async_computation.6 | async-start | bytes 7077888 | tf_op jit(solution)/shard_map/all_to_all | solution.py:143
  227.8 1.5 copy-start.5
  247.9 1.6 copy-start
  248.1 70.4 %collective-permute-start.2 = (f32[1,1,13,49,128]{4,1,3,2,0:T(1,128)S(1)}, f32[1,1,13,49,128]{4,1,3,2,0:T(1,128)S(1)}, u32[]{:S(2)}, u32[]{:S(2)}) collective-permute-start(f32[1,1,13,49,128]{4,1,3,2,0:T(1,128)S(1)} %slice.380), channel_id=1, source_target_pairs={{32,0},{64,32},{96,64},{128,96},{160,128},{192,160},{224,192},{33,... | collective-permute-start | bytes 978440 | tf_op jit(solution)/shard_map/ppermute | solution.py:10
  312.7 21.4 %all-to-all-start.2 = ((bf16[4,2,13824]{2,1,0:T(2,128)(2,1)}), bf16[4,2,13824]{2,1,0:T(2,128)(2,1)}, u32[]{:S(2)}, u32[]{:S(2)}) async-start(bf16[4,2,13824]{2,1,0:T(2,128)(2,1)} %reshape.259), calls=%async_computation.2 | async-start | bytes 442368 | tf_op jit(solution)/shard_map/all_to_all | solution.py:107
  320.8 0.7 copy-start.4
  322.2 15.6 %collective-permute-start.3 = (bf16[1,6,1,49,128]{4,1,3,2,0:T(8,128)(2,1)}, bf16[1,6,1,49,128]{4,1,3,2,0:T(8,128)(2,1)}, u32[]{:S(2)}, u32[]{:S(2)}) collective-permute-start(bf16[1,6,1,49,128]{4,1,3,2,0:T(8,128)(2,1)} %slice.384), channel_id=1, source_target_pairs={{8,0},{16,8},{24,16},{9,1},{17,9},{25,17},{10,2},{18,10},{26,18},{... | collective-permute-start | bytes 225800 | tf_op jit(solution)/shard_map/ppermute | solution.py:10
  334.1 13.9 %all-to-all-start.7 = ((f32[8,1,3456]{2,1,0:T(1,128)}), f32[8,1,3456]{2,1,0:T(1,128)S(1)}, u32[]{:S(2)}, u32[]{:S(2)}) async-start(f32[8,1,3456]{2,1,0:T(1,128)} %reshape.267), calls=%async_computation.7 | async-start | bytes 221184 | tf_op jit(solution)/shard_map/all_to_all | solution.py:146
  337.7 1.3 copy-start.3
Sparse Core Ops, SparseCore 0:
  62.8 88.7 all-gather.1
where the time goes:
time: 364 us; the launch traced here: 358 us
  local copies, waits for them, and re-layouts  113 us (31%)
  starting transfers between devices  80.2 us (22%)
  waiting for transfers between devices  78.5 us (22%)
  blocking collectives  40.2 us (11%)
  matrix products  18.7 us (5%)
  between operations  14.8 us (4%)
  other arithmetic  12.6 us (3%)
    unnamed x66, local copies, waits for them, and re-layouts  67.3 us
    all_to_all x1, waiting for transfers between devices, on_device(): by_filter = lax.all_to_all(taps, ('sy', 'af'), 0, 0, tiled=True).sum(axis=0)  53.2 us
    all_gather x1, blocking collectives, on_device(): kernel_part = lax.all_gather(kernel, ('sy', 'af'), axis=4, tiled=True)  40.2 us
    all_to_all x1, starting transfers between devices, on_device(): lax.all_to_all(grad_after, 'sx', split_axis=1, concat_axis=0, tiled=True)  18.5 us
    dot_general x27, matrix products, spread_back(): lax.dot_general(grad_flat, kernel_full[tap_d, tap_h, tap_w], (((1,), (1,)...  12.4 us
    all_to_all x1, starting transfers between devices, on_device(): lax.all_to_all(lax.all_to_all(grad_after, 'sx', split_axis=1, concat_axis...  12 us
    all_to_all x1, waiting for transfers between devices, on_device(): lax.all_to_all(lax.all_to_all(grad_after, 'sx', split_axis=1, concat_axis...  10.7 us
    all_to_all x1, starting transfers between devices, on_device(): lax.all_to_all(by_sample, 'sx', split_axis=0, concat_axis=1, tiled=True)  9.37 us
  transfers between devices with their start and end apart: 13, of which 6 were waited for; matrix products, arithmetic and copies ran while one was open for 31% of the time, Pallas kernels for 0%

commit v1 on v0

--- a/solution.py
+++ b/solution.py
@@ -1,7 +1,20 @@
+import functools
 import jax
 import jax.numpy as jnp
 from jax import lax
 from jax.sharding import PartitionSpec as P
+
+
+def change_keys(mine_x, ax_name):
+    return jnp.concatenate(
+        lax.all_to_all(
+            jnp.stack(jnp.split(mine_x, lax.axis_size(ax_name), axis=4), axis=0), ax_name, 0, 0
+        ),
+        axis=2,
+    )
+
+
+find_files = functools.partial(change_keys, ax_name="sy")
 
 
 def from_behind(value, axis, steps):
@@ -104,13 +117,7 @@
         samples, depth, height, width, n_sy, n_af, per_dev
     )
     by_sample = lax.all_to_all(conv_space, "af", split_axis=5, concat_axis=0, tiled=True)
-    gathered = lax.all_to_all(
-        lax.all_to_all(by_sample, "sx", split_axis=0, concat_axis=1, tiled=True),
-        "sy",
-        split_axis=4,
-        concat_axis=2,
-        tiled=True,
-    )
+    gathered = find_files(lax.all_to_all(by_sample, "sx", split_axis=0, concat_axis=1, tiled=True))
     own_samples = gathered.shape[0]
     edge_d = gathered.shape[1]
     edge_h = gathered.shape[2]

time: 364 us -> 352 us (0.967)
  the two profiles are of different devices: /device:TPU:96 before, /device:TPU:32 now
where the time goes in v1:
time: 352 us; the launch traced here: 346 us
  waiting for transfers between devices  99.7 us (28%)
  local copies, waits for them, and re-layouts  81.6 us (23%)
  starting transfers between devices  78.7 us (22%)
  blocking collectives  39.2 us (11%)
  matrix products  21.2 us (6%)
  between operations  14.8 us (4%)
  other arithmetic  10.5 us (3%)
    ppermute x4, waiting for transfers between devices, from_behind(): lax.ppermute(value, axis, [(source, source + steps) for source in range(l...  69.9 us
    unnamed x59, local copies, waits for them, and re-layouts  50.1 us
    all_gather x1, blocking collectives, on_device(): kernel_part = lax.all_gather(kernel, ('sy', 'af'), axis=4, tiled=True)  39.2 us
    all_to_all x1, starting transfers between devices, on_device(): lax.all_to_all(grad_after, 'sx', split_axis=1, concat_axis=0, tiled=True)  20.6 us
    dot_general x27, matrix products, spread_back(): lax.dot_general(grad_flat, kernel_full[tap_d, tap_h, tap_w], (((1,), (1,)...  15.4 us
    all_to_all x1, waiting for transfers between devices, on_device(): lax.all_to_all(lax.all_to_all(grad_after, 'sx', split_axis=1, concat_axis...  11 us
    ppermute x4, starting transfers between devices, from_behind(): lax.ppermute(value, axis, [(source, source + steps) for source in range(l...  10.7 us
    all_to_all x1, starting transfers between devices, on_device(): lax.all_to_all(lax.all_to_all(grad_after, 'sx', split_axis=1, concat_axis...  9.57 us
  transfers between devices with their start and end apart: 13, of which 9 were waited for; matrix products, arithmetic and copies ran while one was open for 25% of the time, Pallas kernels for 0%

profile of v1, /device:TPU:32, one launch (start us, length us, event | category | flops | bytes accessed | tf_op | source)
XLA Modules:
  0.0 345.7 jit_solution(1032100684447806204)
XLA Ops:
  9.3 3.4 collective-permute-start
  12.8 6.2 %collective-permute-done = bf16[1,1,12,48,128]{4,1,3,2,0:T(2,128)(2,1)S(1)} collective-permute-done((bf16[1,1,12,48,128]{4,1,3,2,0:T(2,128)(2,1)S(1)}, bf16[1,1,12,48,128]{4,1,3,2,0:T(2,128)(2,1)S(1)}, u32[]{:S(2)}, u32[]{:S(2)}) %collective-permute-start) | collective-permute-done | bytes 147488 | tf_op jit(solution)/shard_map/ppermute | solution.py:23
  19.7 3.8 %collective-permute-start.1 = (bf16[1,7,1,48,128]{4,1,3,2,0:T(8,128)(2,1)}, bf16[1,7,1,48,128]{4,1,3,2,0:T(8,128)(2,1)}, u32[]{:S(2)}, u32[]{:S(2)}) collective-permute-start(bf16[1,7,1,48,128]{4,1,3,2,0:T(8,128)(2,1)} %pad_maximum_fusion.10), channel_id=1, source_target_pairs={{0,8},{8,16},{16,24},{1,9},{9,17},{17,25},{2,10},{10,18},{18,26},{... | collective-permute-start | bytes 258056 | tf_op jit(solution)/shard_map/ppermute | solution.py:23
  23.6 39.2 %all_gather.6 = bf16[3,3,3,16,256]{3,4,2,1,0:T(8,128)(2,1)S(1)} all-gather(bf16[3,3,3,16,8]{3,4,2,1,0:T(8,128)(2,1)S(1)} %copy-done.5), channel_id=1, replica_groups=mesh['sx'=8,'sy'=4,'af'=8] {'sy','af'}, dimensions={4}, use_global_device_ids=true | all-gather | bytes 228096 | tf_op jit(solution)/shard_map/all_gather | solution.py:102
  69.2 20.6 %all-to-all-start.3 = ((bf16[8,2,6912]{2,1,0:T(2,128)(2,1)}), bf16[8,2,6912]{2,1,0:T(2,128)(2,1)S(1)}, u32[]{:S(2)}, u32[]{:S(2)}) async-start(bf16[8,2,6912]{2,1,0:T(2,128)(2,1)} %reshape.260), calls=%async_computation.3 | async-start | bytes 442368 | tf_op jit(solution)/shard_map/all_to_all | solution.py:135
  116.4 9.6 %all-to-all-start.4 = ((bf16[4,2,13824]{2,1,0:T(2,128)(2,1)}), bf16[4,2,13824]{2,1,0:T(2,128)(2,1)S(1)}, u32[]{:S(2)}, u32[]{:S(2)}) async-start(bf16[4,2,13824]{2,1,0:T(2,128)(2,1)} %reshape.262), calls=%async_computation.4 | async-start | bytes 442368 | tf_op jit(solution)/shard_map/all_to_all | solution.py:134
  127.5 11.0 %all-to-all-done.4 = bf16[4,2,13824]{2,1,0:T(2,128)(2,1)S(1)} async-done(((bf16[4,2,13824]{2,1,0:T(2,128)(2,1)}), bf16[4,2,13824]{2,1,0:T(2,128)(2,1)S(1)}, u32[]{:S(2)}, u32[]{:S(2)}) %all-to-all-start.4) | async-done | bytes 221216 | tf_op jit(solution)/shard_map/all_to_all | solution.py:134
  142.7 8.4 %all-to-all-start.5 = ((bf16[8,2,6912]{2,1,0:T(2,128)(2,1)}), bf16[8,2,6912]{2,1,0:T(2,128)(2,1)S(1)}, u32[]{:S(2)}, u32[]{:S(2)}) async-start(bf16[8,2,6912]{2,1,0:T(2,128)(2,1)} %reshape.264), calls=%async_computation.5 | async-start | bytes 442368 | tf_op jit(solution)/shard_map/all_to_all | solution.py:141
  154.3 3.6 %dot_general.205 = bf16[27,128,432]{1,0,2:T(8,128)(2,1)} reshape(bf16[3456,432]{0,1:T(8,128)(2,1)S(1)} %bitcast.447) | data formatting | bytes 5971968 | tf_op jit(solution)/shard_map/dot_general | solution.py:144
  158.2 2.7 reshape.265
  165.8 3.5 %reshape.254 = bf16[8,2,6912]{2,1,0:T(2,128)(2,1)} reshape(bf16[8,1,3,6,4,8,24]{6,5,4,3,2,1,0:T(8,128)(2,1)} %bitcast.459) | data formatting | bytes 442368
  169.4 4.5 %all-to-all-start = ((bf16[8,2,6912]{2,1,0:T(2,128)(2,1)}), bf16[8,2,6912]{2,1,0:T(2,128)(2,1)S(1)}, u32[]{:S(2)}, u32[]{:S(2)}) async-start(bf16[8,2,6912]{2,1,0:T(2,128)(2,1)} %reshape.254), calls=%async_computation | async-start | bytes 442368 | tf_op jit(solution)/shard_map/all_to_all | solution.py:119
  176.3 4.7 %all-to-all-done = bf16[8,2,6912]{2,1,0:T(2,128)(2,1)S(1)} async-done(((bf16[8,2,6912]{2,1,0:T(2,128)(2,1)}), bf16[8,2,6912]{2,1,0:T(2,128)(2,1)S(1)}, u32[]{:S(2)}, u32[]{:S(2)}) %all-to-all-start) | async-done | bytes 221216 | tf_op jit(solution)/shard_map/all_to_all | solution.py:119
  185.1 8.0 %all-to-all-start.1 = ((bf16[8,2,6912]{2,1,0:T(2,128)(2,1)}), bf16[8,2,6912]{2,1,0:T(2,128)(2,1)S(1)}, u32[]{:S(2)}, u32[]{:S(2)}) async-start(bf16[8,2,6912]{2,1,0:T(2,128)(2,1)} %reshape.256), calls=%async_computation.1 | async-start | bytes 442368 | tf_op jit(solution)/shard_map/all_to_all | solution.py:120
  193.1 3.4 fusion.6
  196.5 3.8 %copy.666 = f32[32,27,128,8]{2,3,1,0:T(8,128)} copy(f32[32,27,128,8]{2,0,3,1:T(8,128)S(1)} %fusion.6) | data formatting | bytes 7077888 | tf_op jit(solution)/shard_map/transpose | solution.py:149
  201.6 2.5 all-to-all-done.1
  208.5 6.1 %all-to-all-start.2 = ((bf16[4,2,13824]{2,1,0:T(2,128)(2,1)}), bf16[4,2,13824]{2,1,0:T(2,128)(2,1)S(1)}, u32[]{:S(2)}, u32[]{:S(2)}) async-start(bf16[4,2,13824]{2,1,0:T(2,128)(2,1)} %reshape.258), calls=%async_computation.2 | async-start | bytes 442368 | tf_op jit(solution)/shard_map/all_to_all | solution.py:10
  217.7 2.8 all-to-all-done.2
  220.5 5.4 %all-to-all-start.6 = ((f32[32,27,128,8]{2,3,1,0:T(8,128)}), f32[32,27,128,8]{2,3,1,0:T(8,128)}, u32[]{:S(2)}, u32[]{:S(2)}) async-start(f32[32,27,128,8]{2,3,1,0:T(8,128)} %copy.666), calls=%async_computation.6 | async-start | bytes 7077888 | tf_op jit(solution)/shard_map/all_to_all | solution.py:150
  245.9 10.1 %collective-permute-done.2 = f32[1,1,13,49,128]{4,1,3,2,0:T(1,128)S(1)} collective-permute-done((f32[1,1,13,49,128]{4,1,3,2,0:T(1,128)S(1)}, f32[1,1,13,49,128]{4,1,3,2,0:T(1,128)S(1)}, u32[]{:S(2)}, u32[]{:S(2)}) %collective-permute-start.2) | collective-permute-done | bytes 326176 | tf_op jit(solution)/shard_map/ppermute | solution.py:23
  259.6 53.6 %collective-permute-done.3 = bf16[1,6,1,49,128]{4,1,3,2,0:T(8,128)(2,1)S(1)} collective-permute-done((bf16[1,6,1,49,128]{4,1,3,2,0:T(8,128)(2,1)S(1)}, bf16[1,6,1,49,128]{4,1,3,2,0:T(8,128)(2,1)S(1)}, u32[]{:S(2)}, u32[]{:S(2)}) %collective-permute-start.3) | collective-permute-done | bytes 75296 | tf_op jit(solution)/shard_map/ppermute | solution.py:23
  320.5 5.2 %all-to-all-start.7 = ((f32[8,1,3456]{2,1,0:T(1,128)}), f32[8,1,3456]{2,1,0:T(1,128)S(1)}, u32[]{:S(2)}, u32[]{:S(2)}) async-start(f32[8,1,3456]{2,1,0:T(1,128)} %reshape.266), calls=%async_computation.7 | async-start | bytes 221184 | tf_op jit(solution)/shard_map/all_to_all | solution.py:153
  327.5 8.5 %all-to-all-done.7 = f32[8,1,3456]{2,1,0:T(1,128)S(1)} async-done(((f32[8,1,3456]{2,1,0:T(1,128)}), f32[8,1,3456]{2,1,0:T(1,128)S(1)}, u32[]{:S(2)}, u32[]{:S(2)}) %all-to-all-start.7) | async-done | bytes 110624 | tf_op jit(solution)/shard_map/all_to_all | solution.py:153
  (152 shorter events, 100.2 us)
Async XLA Ops:
  7.2 16.4 %copy-start.5 = (bf16[3,3,3,16,8]{3,4,2,1,0:T(8,128)(2,1)S(1)}, bf16[3,3,3,16,8]{3,4,2,1,0:T(8,128)(2,1)}, u32[]{:S(2)}) copy-start(bf16[3,3,3,16,8]{3,4,2,1,0:T(8,128)(2,1)} %param.4) | copy-start | bytes 20740
  7.2 153.7 %all-gather.2.cloned.1.call-start = ((), (), s32[]{:S(2)}) async-start(), calls=%async_computation.8 | async-start | bytes 1990656 | tf_op jit(solution)/shard_map/all_gather | solution.py:103
  9.3 9.7 %collective-permute-start = (bf16[1,1,12,48,128]{4,1,3,2,0:T(2,128)(2,1)S(1)}, bf16[1,1,12,48,128]{4,1,3,2,0:T(2,128)(2,1)S(1)}, u32[]{:S(2)}, u32[]{:S(2)}) collective-permute-start(bf16[1,1,12,48,128]{4,1,3,2,0:T(2,128)(2,1)S(1)} %slice.315), channel_id=1, source_target_pairs={{0,32},{32,64},{64,96},{96,128},{128,160},{160,192},{192,224},{1,3... | collective-permute-start | bytes 442376 | tf_op jit(solution)/shard_map/ppermute | solution.py:23
  19.0 0.7 copy-start.2
  19.7 70.1 %collective-permute-start.1 = (bf16[1,7,1,48,128]{4,1,3,2,0:T(8,128)(2,1)}, bf16[1,7,1,48,128]{4,1,3,2,0:T(8,128)(2,1)}, u32[]{:S(2)}, u32[]{:S(2)}) collective-permute-start(bf16[1,7,1,48,128]{4,1,3,2,0:T(8,128)(2,1)} %pad_maximum_fusion.10), channel_id=1, source_target_pairs={{0,8},{8,16},{16,24},{1,9},{9,17},{17,25},{2,10},{10,18},{18,26},{... | collective-permute-start | bytes 258056 | tf_op jit(solution)/shard_map/ppermute | solution.py:23
  67.0 22.9 %copy-start.3 = (bf16[1,1,12,48,128]{4,1,3,2,0:T(2,128)(2,1)S(1)}, bf16[1,1,12,48,128]{4,1,3,2,0:T(2,128)(2,1)}, u32[]{:S(2)}) copy-start(bf16[1,1,12,48,128]{4,1,3,2,0:T(2,128)(2,1)} %copy-done.2) | copy-start | bytes 442372
  69.2 42.9 %all-to-all-start.3 = ((bf16[8,2,6912]{2,1,0:T(2,128)(2,1)}), bf16[8,2,6912]{2,1,0:T(2,128)(2,1)S(1)}, u32[]{:S(2)}, u32[]{:S(2)}) async-start(bf16[8,2,6912]{2,1,0:T(2,128)(2,1)} %reshape.260), calls=%async_computation.3 | async-start | bytes 442368 | tf_op jit(solution)/shard_map/all_to_all | solution.py:135
  116.4 22.1 %all-to-all-start.4 = ((bf16[4,2,13824]{2,1,0:T(2,128)(2,1)}), bf16[4,2,13824]{2,1,0:T(2,128)(2,1)S(1)}, u32[]{:S(2)}, u32[]{:S(2)}) async-start(bf16[4,2,13824]{2,1,0:T(2,128)(2,1)} %reshape.262), calls=%async_computation.4 | async-start | bytes 442368 | tf_op jit(solution)/shard_map/all_to_all | solution.py:134
  142.7 15.5 %all-to-all-start.5 = ((bf16[8,2,6912]{2,1,0:T(2,128)(2,1)}), bf16[8,2,6912]{2,1,0:T(2,128)(2,1)S(1)}, u32[]{:S(2)}, u32[]{:S(2)}) async-start(bf16[8,2,6912]{2,1,0:T(2,128)(2,1)} %reshape.264), calls=%async_computation.5 | async-start | bytes 442368 | tf_op jit(solution)/shard_map/all_to_all | solution.py:141
  164.5 9.4 %copy-start = (bf16[8,1,3,4,6,8,24]{6,5,4,3,2,1,0:T(8,128)(2,1)S(1)}, bf16[8,1,3,4,6,8,24]{6,5,4,3,2,1,0:T(8,128)(2,1)}, u32[]{:S(2)}) copy-start(bf16[8,1,3,4,6,8,24]{6,5,4,3,2,1,0:T(8,128)(2,1)} %reshape.265) | copy-start | bytes 663556
  169.4 11.6 %all-to-all-start = ((bf16[8,2,6912]{2,1,0:T(2,128)(2,1)}), bf16[8,2,6912]{2,1,0:T(2,128)(2,1)S(1)}, u32[]{:S(2)}, u32[]{:S(2)}) async-start(bf16[8,2,6912]{2,1,0:T(2,128)(2,1)} %reshape.254), calls=%async_computation | async-start | bytes 442368 | tf_op jit(solution)/shard_map/all_to_all | solution.py:119
  182.9 10.2 %copy-start.4 = (bf16[432,256]{0,1:T(8,128)(2,1)S(1)}, bf16[432,256]{0,1:T(8,128)(2,1)}, u32[]{:S(2)}) copy-start(bf16[432,256]{0,1:T(8,128)(2,1)} %reshape_reshape.8) | copy-start | bytes 663556
  185.1 18.9 %all-to-all-start.1 = ((bf16[8,2,6912]{2,1,0:T(2,128)(2,1)}), bf16[8,2,6912]{2,1,0:T(2,128)(2,1)S(1)}, u32[]{:S(2)}, u32[]{:S(2)}) async-start(bf16[8,2,6912]{2,1,0:T(2,128)(2,1)} %reshape.256), calls=%async_computation.1 | async-start | bytes 442368 | tf_op jit(solution)/shard_map/all_to_all | solution.py:120
  208.5 8.1 %copy-start.1 = (bf16[3,3,3,128,256]{4,3,2,1,0:T(8,128)(2,1)S(1)}, bf16[3,3,3,128,256]{4,3,2,1,0:T(8,128)(2,1)}, u32[]{:S(2)}) copy-start(bf16[3,3,3,128,256]{4,3,2,1,0:T(8,128)(2,1)} %all-gather.2.cloned.1.call-done) | copy-start | bytes 5308420
  208.5 12.0 %all-to-all-start.2 = ((bf16[4,2,13824]{2,1,0:T(2,128)(2,1)}), bf16[4,2,13824]{2,1,0:T(2,128)(2,1)S(1)}, u32[]{:S(2)}, u32[]{:S(2)}) async-start(bf16[4,2,13824]{2,1,0:T(2,128)(2,1)} %reshape.258), calls=%async_computation.2 | async-start | bytes 442368 | tf_op jit(solution)/shard_map/all_to_all | solution.py:10
  220.5 95.7 %all-to-all-start.6 = ((f32[32,27,128,8]{2,3,1,0:T(8,128)}), f32[32,27,128,8]{2,3,1,0:T(8,128)}, u32[]{:S(2)}, u32[]{:S(2)}) async-start(f32[32,27,128,8]{2,3,1,0:T(8,128)} %copy.666), calls=%async_computation.6 | async-start | bytes 7077888 | tf_op jit(solution)/shard_map/all_to_all | solution.py:150
  244.4 11.6 %collective-permute-start.2 = (f32[1,1,13,49,128]{4,1,3,2,0:T(1,128)S(1)}, f32[1,1,13,49,128]{4,1,3,2,0:T(1,128)S(1)}, u32[]{:S(2)}, u32[]{:S(2)}) collective-permute-start(f32[1,1,13,49,128]{4,1,3,2,0:T(1,128)S(1)} %slice.380), channel_id=1, source_target_pairs={{32,0},{64,32},{96,64},{128,96},{160,128},{192,160},{224,192},{33,... | collective-permute-start | bytes 978440 | tf_op jit(solution)/shard_map/ppermute | solution.py:23
  257.1 56.0 %collective-permute-start.3 = (bf16[1,6,1,49,128]{4,1,3,2,0:T(8,128)(2,1)S(1)}, bf16[1,6,1,49,128]{4,1,3,2,0:T(8,128)(2,1)S(1)}, u32[]{:S(2)}, u32[]{:S(2)}) collective-permute-start(bf16[1,6,1,49,128]{4,1,3,2,0:T(8,128)(2,1)S(1)} %slice.384), channel_id=1, source_target_pairs={{8,0},{16,8},{24,16},{9,1},{17,9},{25,17},{10,2},{18,10},{26,18},{... | collective-permute-start | bytes 225800 | tf_op jit(solution)/shard_map/ppermute | solution.py:23
  320.5 15.6 %all-to-all-start.7 = ((f32[8,1,3456]{2,1,0:T(1,128)}), f32[8,1,3456]{2,1,0:T(1,128)S(1)}, u32[]{:S(2)}, u32[]{:S(2)}) async-start(f32[8,1,3456]{2,1,0:T(1,128)} %reshape.266), calls=%async_computation.7 | async-start | bytes 221184 | tf_op jit(solution)/shard_map/all_to_all | solution.py:153
Sparse Core Ops, SparseCore 0:
  64.3 89.6 all-gather.1
